TPU v7x, 32 devices: a whole 2x2x4 slice. The times are simulated.
32 devices in a mesh: ia: 8 (over y, x, core), ja: 4 (over z).
Axes of the slice: x: 2, y: 2, z: 4, core: 2. Of those that a mesh axis runs over, the one named last changes fastest.
Arguments:
- slabs: bfloat16 [32, 512, 512], P(('ia', 'ja')), may hold values from -1.1953125 to 1.1953125
- pno_coef: bfloat16 [512, 256, 128], P(('ia', 'ja')), may hold values from -0.375 to 0.375
- dom_blocks: int32 [512, 2], P(('ia', 'ja')), may hold values from 0 to 3, as said below
- pair_first: int32 [512], P(('ia', 'ja')), may hold values from 0 to 3
- pair_second: int32 [512], P(('ia', 'ja')), may hold values from 0 to 7
- pno_energy: float32 [512, 128], P(('ia', 'ja')), may hold values from 0.3 to 3
- pair_shift: float32 [512], P(('ia', 'ja')), may hold values from 0.5 to 2
- margin_i: bfloat16 [512, 16, 128, 128], P(('ia', 'ja')), may hold values from -0.5 to 0.5
- margin_j: bfloat16 [512, 16, 128, 128], P(('ia', 'ja')), may hold values from -0.5 to 0.5
- couple_i: float32 [512, 16], P(('ia', 'ja')), may hold values from -0.45 to 0.45
- couple_j: float32 [512, 16], P(('ia', 'ja')), may hold values from -0.45 to 0.45
- ask_i: int32 [32, 8, 4], P(('ia', 'ja')), may hold values from 0 to 15, as said below
- ask_j: int32 [32, 4, 4], P(('ia', 'ja')), may hold values from 0 to 15, as said below
- link_i: int32 [512, 16], P(('ia', 'ja')), may hold values from 0 to 31, as said below
- link_j: int32 [512, 16], P(('ia', 'ja')), may hold values from 0 to 15, as said below
Outputs:
- amplitudes: float32 [512, 128, 128], P(('ia', 'ja'))
- density: float32 [512, 512], P(('ia', 'ja'))
Inputs may be any that keep to these rules, and one draw needn't show every extreme that they name: `dom_blocks`: the 2 blocks of a pair are distinct. `ask_i`: for each block g and each peer s, the 4 slots are distinct. `ask_j`: for each block g and each peer s, the 4 slots are distinct. `link_i`: within each aligned block of 16 pairs every value is named at least once. `link_j`: within each aligned block of 16 pairs every value is named at least once.
All inputs are finite; a program needn't handle non-finite values.
Results may differ from a plain program's by a relative error of at most 0.0045.
Values may be sent and summed in bfloat16 or wider, within the bound.
A program may use at most 128 MiB of HBM per device.

v0:
```python
import math
import jax
import jax.numpy as jnp
from jax import lax
from jax.sharding import PartitionSpec as P

BLK = 128
ITERS = 2


def coupled(near_blocks, margin_blocks, weights):
    left_side = jnp.einsum(
        "pnab,pnbc->pnac", margin_blocks, near_blocks, preferred_element_type=jnp.float32
    ).astype(jnp.bfloat16)
    product = jnp.einsum(
        "pnac,pndc->pnad", left_side, margin_blocks, preferred_element_type=jnp.float32
    )
    return jnp.sum(weights[:, :, None, None] * product, axis=1)


def body(
    slabs,
    pno_coef,
    dom_blocks,
    pair_first,
    pair_second,
    pno_energy,
    pair_shift,
    margin_i,
    margin_j,
    couple_i,
    couple_j,
    ask_i,
    ask_j,
    link_i,
    link_j,
):
    pair_count = pno_coef.shape[0]
    pno_count = pno_coef.shape[2]
    pao_count = slabs.shape[1]
    aux_count = slabs.shape[2]
    block_count = pao_count // BLK
    domain_count = dom_blocks.shape[1]
    row_peers = lax.axis_size("ia")
    col_peers = lax.axis_size("ja")
    row_slots = ask_i.shape[2]
    col_slots = ask_j.shape[2]
    row_slabs = lax.all_gather(slabs, "ja", axis=0, tiled=True)
    col_slabs = lax.all_gather(slabs, "ia", axis=0, tiled=True)
    rows_first = row_slabs.reshape(-1, BLK, aux_count)[
        pair_first[:, None] * block_count + dom_blocks
    ].reshape(pair_count, -1, aux_count)
    rows_second = col_slabs.reshape(-1, BLK, aux_count)[
        pair_second[:, None] * block_count + dom_blocks
    ].reshape(pair_count, -1, aux_count)
    projected_first = jnp.einsum(
        "pmn,pmq->pnq", pno_coef, rows_first, preferred_element_type=jnp.float32
    ).astype(jnp.bfloat16)
    projected_second = jnp.einsum(
        "pmn,pmq->pnq", pno_coef, rows_second, preferred_element_type=jnp.float32
    ).astype(jnp.bfloat16)
    exchange_ints = jnp.einsum(
        "paq,pbq->pab", projected_first, projected_second, preferred_element_type=jnp.float32
    )
    denominator = pno_energy[:, :, None] + pno_energy[:, None, :] + pair_shift[:, None, None]
    amplitudes = -exchange_ints / denominator
    asked_rows = lax.all_to_all(ask_i, "ia", split_axis=1, concat_axis=0, tiled=True).reshape(
        row_peers, row_slots
    )
    asked_cols = lax.all_to_all(ask_j, "ja", split_axis=1, concat_axis=0, tiled=True).reshape(
        col_peers, col_slots
    )
    for iteration in range(ITERS):
        sent = amplitudes.astype(jnp.bfloat16)
        table_rows = lax.all_to_all(
            sent[asked_rows], "ia", split_axis=0, concat_axis=0, tiled=True
        ).reshape(-1, pno_count, pno_count)
        table_cols = lax.all_to_all(
            sent[asked_cols], "ja", split_axis=0, concat_axis=0, tiled=True
        ).reshape(-1, pno_count, pno_count)
        near_rows = table_rows[link_i]
        near_cols = table_cols[link_j]
        coupling = coupled(near_rows, margin_i, couple_i) + coupled(near_cols, margin_j, couple_j)
        residual = exchange_ints + denominator * amplitudes + coupling
        amplitudes = amplitudes - residual / denominator
    sent = amplitudes.astype(jnp.bfloat16)
    square = (
        jnp.einsum("pab,pcb->pac", sent, sent, preferred_element_type=jnp.float32)
        + jnp.einsum("pba,pbc->pac", sent, sent, preferred_element_type=jnp.float32)
    ).astype(jnp.bfloat16)
    mapped = jnp.einsum(
        "pmn,pnk->pmk", pno_coef, square, preferred_element_type=jnp.float32
    ).astype(jnp.bfloat16)
    mapped_blocks = mapped.reshape(pair_count, domain_count, BLK, pno_count)
    coef_blocks = pno_coef.reshape(pair_count, domain_count, BLK, pno_count)
    domain_density = jnp.einsum(
        "pkrn,plcn->pklrc", mapped_blocks, coef_blocks, preferred_element_type=jnp.float32
    )
    select = (
        dom_blocks[:, :, None] == jnp.arange(block_count, dtype=jnp.int32)[None, None, :]
    ).astype(jnp.float32)
    placement = jnp.einsum("pkg,plh->ghpkl", select, select).reshape(
        block_count * block_count, pair_count * domain_count * domain_count
    )
    stacked = jnp.dot(
        placement,
        domain_density.reshape(pair_count * domain_count * domain_count, BLK * BLK),
        precision=lax.Precision.HIGHEST,
        preferred_element_type=jnp.float32,
    )
    partial_sum = (
        stacked.reshape(block_count, block_count, BLK, BLK)
        .transpose(0, 2, 1, 3)
        .reshape(pao_count, pao_count)
    )
    all_devices = lax.axis_size(("ia", "ja"))
    factor = 1.0 / math.sqrt(pair_count * all_devices)
    owned_rows = pao_count // all_devices
    summed = lax.psum(partial_sum, ("ia", "ja"))
    owned = lax.dynamic_slice_in_dim(
        summed, lax.axis_index(("ia", "ja")) * owned_rows, owned_rows, 0
    )
    return (amplitudes, owned * factor)


def solution(mesh):
    in_specs = (
        P(("ia", "ja"), None, None),
        P(("ia", "ja"), None, None),
        P(("ia", "ja"), None),
        P(("ia", "ja")),
        P(("ia", "ja")),
        P(("ia", "ja"), None),
        P(("ia", "ja")),
        P(("ia", "ja"), None, None, None),
        P(("ia", "ja"), None, None, None),
        P(("ia", "ja"), None),
        P(("ia", "ja"), None),
        P(("ia", "ja"), None, None),
        P(("ia", "ja"), None, None),
        P(("ia", "ja"), None),
        P(("ia", "ja"), None),
    )
    out_specs = (P(("ia", "ja"), None, None), P(("ia", "ja"), None))
    return jax.shard_map(body, mesh=mesh, in_specs=in_specs, out_specs=out_specs, check_vma=False)
```

profile of v0, /device:TPU:0, one launch (start us, length us, event | category | flops | bytes accessed | tf_op | source)
XLA Modules:
  0.0 441.4 jit_solution(10866756121001546754)
XLA Ops:
  8.7 6.4 %all-to-all-start.2 = ((s32[1,4,4]{2,0,1:T(1,128)}), s32[1,4,4]{2,0,1:T(1,128)S(1)}, u32[]{:S(2)}, u32[]{:S(2)}) async-start(s32[1,4,4]{2,0,1:T(1,128)} %bitcast.108), calls=%async_computation.2 | async-start | bytes 4096 | tf_op jit(solution)/shard_map/all_to_all | solution.py:70
  18.1 2.4 all-to-all-done.2
  20.5 3.7 all-to-all-start
  24.3 33.6 %all-gather.3.cloned.1.call-done = bf16[4,512,512]{2,1,0:T(8,128)(2,1)} async-done(((bf16[1,512,512]{2,1,0:T(8,128)(2,1)}), bf16[4,512,512]{2,1,0:T(8,128)(2,1)}) %all-gather.3.cloned.1.call-update) | async-done | bytes 2097168 | tf_op jit(solution)/shard_map/all_gather | solution.py:48
  58.0 4.4 %gather_fusion = bf16[32,128,512]{2,1,0:T(8,128)(2,1)} fusion(bf16[16,128,512]{2,1,0:T(8,128)(2,1)} %bitcast.93, s32[1024]{0:T(1024)S(1)} %pad_clamp_fusion.5), kind=kCustom, calls=%fused_computation | custom fusion | bytes 8388736 | tf_op jit(solution)/shard_map/gather | solution.py:50
  62.4 32.9 %all-gather.5.cloned.1.call-done = bf16[8,512,512]{2,1,0:T(8,128)(2,1)} async-done(((bf16[1,512,512]{2,1,0:T(8,128)(2,1)}), bf16[8,512,512]{2,1,0:T(8,128)(2,1)}) %all-gather.5.cloned.1.call-update) | async-done | bytes 4194320 | tf_op jit(solution)/shard_map/all_gather | solution.py:49
  95.3 5.0 %gather_fusion.1 = bf16[32,128,512]{2,1,0:T(8,128)(2,1)} fusion(bf16[32,128,512]{2,1,0:T(8,128)(2,1)} %bitcast.98, s32[1024]{0:T(1024)S(1)} %pad_clamp_fusion.4), kind=kCustom, calls=%fused_computation.1 | custom fusion | bytes 8388736 | tf_op jit(solution)/shard_map/gather | solution.py:53
  100.3 7.5 %fusion.36 = (bf16[16,128,128]{2,1,0:T(8,128)(2,1)S(1)}, f32[16,128,128]{2,1,0:T(8,128)}) fusion(f32[16]{0:T(128)S(1)} %copy-done.8, f32[16,128]{1,0:T(8,128)S(1)} %copy-done.4, bf16[16,256,512]{2,1,0:T(8,128)(2,1)} %bitcast.100, bf16[16,256,128]{2,1,0:T(8,128)(2,1)S(1)} %copy-done, bf16[16,256,512]{2,1,0:T(8,128)(2,1)} %bitcast.99), kind=kOutput, calls=%fused_computation.44 | convolution fusion | flops 1345585152 | bytes 11018304 | tf_op jit(solution)/shard_map/paq,pbq->pab/dot_general | solution.py:62
  107.8 1.4 gather_fusion.4
  109.2 4.6 %all-to-all-start.3 = ((bf16[4,4,128,128]{3,2,1,0:T(8,128)(2,1)}), bf16[4,4,128,128]{3,2,1,0:T(8,128)(2,1)S(1)}, u32[]{:S(2)}, u32[]{:S(2)}) async-start(bf16[4,4,128,128]{3,2,1,0:T(8,128)(2,1)} %bitcast.10), calls=%async_computation.3 | async-start | bytes 1048576 | tf_op jit(solution)/shard_map/all_to_all | solution.py:78
  114.3 1.7 gather_fusion.2
  116.0 12.8 %all-to-all-done.3 = bf16[4,4,128,128]{3,2,1,0:T(8,128)(2,1)S(1)} async-done(((bf16[4,4,128,128]{3,2,1,0:T(8,128)(2,1)}), bf16[4,4,128,128]{3,2,1,0:T(8,128)(2,1)S(1)}, u32[]{:S(2)}, u32[]{:S(2)}) %all-to-all-start.3) | async-done | bytes 524320 | tf_op jit(solution)/shard_map/all_to_all | solution.py:78
  128.7 3.9 all-to-all-start.1
  132.7 8.6 %gather_fusion.5 = bf16[256,128,128]{2,1,0:T(8,128)(2,1)} fusion(bf16[16,128,128]{2,1,0:T(8,128)(2,1)S(1)} %bitcast.88, s32[1024]{0:T(1024)S(1)} %pad_clamp_fusion), kind=kCustom, calls=%fused_computation.5 | custom fusion | bytes 16778240 | tf_op jit(solution)/shard_map/gather | solution.py:82
  141.3 20.5 %multiply_reduce_fusion.2 = f32[16,128,128]{2,1,0:T(8,128)} fusion(f32[16,16]{1,0:T(8,128)S(1)} %copy-done.9, bf16[16,16,128,128]{3,2,1,0:T(8,128)(2,1)} %param.23, bf16[16,16,128,128]{3,2,1,0:T(8,128)(2,1)} %bitcast.96), kind=kOutput, calls=%fused_computation.12 | convolution fusion | flops 2159804416 | bytes 17826816 | tf_op jit(solution)/shard_map/pnac,pndc->pnad/dot_general | solution.py:15
  161.8 8.6 %gather_fusion.3 = bf16[256,128,128]{2,1,0:T(8,128)(2,1)} fusion(bf16[32,128,128]{2,1,0:T(8,128)(2,1)S(1)} %bitcast.91, s32[1024]{0:T(1024)S(1)} %pad_clamp_fusion.2), kind=kCustom, calls=%fused_computation.3 | custom fusion | bytes 16778240 | tf_op jit(solution)/shard_map/gather | solution.py:81
  170.5 32.2 %multiply_reduce_fusion.3 = f32[16,128,128]{2,1,0:T(8,128)} fusion(f32[16,16]{1,0:T(8,128)S(1)} %copy-done.10, bf16[16,16,128,128]{3,2,1,0:T(8,128)(2,1)} %param.22, bf16[16,16,128,128]{3,2,1,0:T(8,128)(2,1)} %bitcast.97), kind=kOutput, calls=%fused_computation.13 | convolution fusion | flops 2159804416 | bytes 17826816 | tf_op jit(solution)/shard_map/pnac,pndc->pnad/dot_general | solution.py:15
  202.7 3.1 fusion.42
  207.2 3.5 all-to-all-start.5
  211.2 1.7 gather_fusion.6
  212.9 13.1 %all-to-all-done.5 = bf16[4,4,128,128]{3,2,1,0:T(8,128)(2,1)S(1)} async-done(((bf16[4,4,128,128]{3,2,1,0:T(8,128)(2,1)}), bf16[4,4,128,128]{3,2,1,0:T(8,128)(2,1)S(1)}, u32[]{:S(2)}, u32[]{:S(2)}) %all-to-all-start.5) | async-done | bytes 524320 | tf_op jit(solution)/shard_map/all_to_all | solution.py:78
  226.0 3.8 all-to-all-start.4
  229.9 8.6 %gather_fusion.9 = bf16[256,128,128]{2,1,0:T(8,128)(2,1)} fusion(bf16[16,128,128]{2,1,0:T(8,128)(2,1)S(1)} %bitcast.89, s32[1024]{0:T(1024)S(1)} %pad_clamp_fusion), kind=kCustom, calls=%fused_computation.9 | custom fusion | bytes 16778240 | tf_op jit(solution)/shard_map/gather | solution.py:82
  238.6 20.5 %multiply_reduce_fusion = f32[16,128,128]{2,1,0:T(8,128)} fusion(f32[16,16]{1,0:T(8,128)S(1)} %copy-done.9, bf16[16,16,128,128]{3,2,1,0:T(8,128)(2,1)} %param.23, bf16[16,16,128,128]{3,2,1,0:T(8,128)(2,1)} %bitcast.94), kind=kOutput, calls=%fused_computation.10 | convolution fusion | flops 2159804416 | bytes 17826816 | tf_op jit(solution)/shard_map/pnac,pndc->pnad/dot_general | solution.py:15
  259.1 8.6 %gather_fusion.7 = bf16[256,128,128]{2,1,0:T(8,128)(2,1)} fusion(bf16[32,128,128]{2,1,0:T(8,128)(2,1)S(1)} %bitcast.90, s32[1024]{0:T(1024)S(1)} %pad_clamp_fusion.2), kind=kCustom, calls=%fused_computation.7 | custom fusion | bytes 16778240 | tf_op jit(solution)/shard_map/gather | solution.py:81
  267.7 20.5 %multiply_reduce_fusion.1 = f32[16,128,128]{2,1,0:T(8,128)} fusion(f32[16,16]{1,0:T(8,128)S(1)} %copy-done.10, bf16[16,16,128,128]{3,2,1,0:T(8,128)(2,1)} %param.22, bf16[16,16,128,128]{3,2,1,0:T(8,128)(2,1)} %bitcast.95), kind=kOutput, calls=%fused_computation.11 | convolution fusion | flops 2159804416 | bytes 17826816 | tf_op jit(solution)/shard_map/pnac,pndc->pnad/dot_general | solution.py:15
  288.3 2.4 divide_subtract_fusion
  290.7 1.5 fusion.39
  292.1 1.9 fusion.33
  295.3 1.9 fusion.43
  297.3 4.6 %fusion.16 = f32[4,4,128,128]{3,1,2,0:T(4,128)S(1)} fusion(f32[4,4,64,1]{1,2,3,0:T(8,128)S(1)} %bitcast.106, f32[8,8,128,128]{3,2,1,0:T(8,128)S(1)} %bitcast.92), kind=kOutput, calls=%fused_computation.28 | convolution fusion | flops 201326592 | bytes 5246976 | tf_op jit(solution)/shard_map/dot_general | solution.py:105
  302.9 130.3 %all-reduce.2.cloned.1.call-done = f32[512,512]{1,0:T(8,128)} async-done(((f32[512,512]{1,0:T(8,128)}), f32[512,512]{1,0:T(8,128)}) %all-reduce.2.cloned.1.call-update) | async-done | bytes 1048592 | tf_op jit(solution)/shard_map/psum | solution.py:119
  (62 shorter events, 10.8 us)
Async XLA Ops:
  7.2 93.1 %copy-start = (bf16[16,256,128]{2,1,0:T(8,128)(2,1)S(1)}, bf16[16,256,128]{2,1,0:T(8,128)(2,1)}, u32[]{:S(2)}) copy-start(bf16[16,256,128]{2,1,0:T(8,128)(2,1)} %param.16) | copy-start | bytes 3145732
  7.2 50.8 %all-gather.3.cloned.1.call-start = ((), (), s32[]{:S(2)}) async-start(), calls=%async_computation.6 | async-start | bytes 2621440 | tf_op jit(solution)/shard_map/all_gather | solution.py:48
  7.9 87.4 %all-gather.5.cloned.1.call-start = ((), (), s32[]{:S(2)}) async-start(), calls=%async_computation.7 | async-start | bytes 4718592 | tf_op jit(solution)/shard_map/all_gather | solution.py:49
  8.7 11.9 %all-to-all-start.2 = ((s32[1,4,4]{2,0,1:T(1,128)}), s32[1,4,4]{2,0,1:T(1,128)S(1)}, u32[]{:S(2)}, u32[]{:S(2)}) async-start(s32[1,4,4]{2,0,1:T(1,128)} %bitcast.108), calls=%async_computation.2 | async-start | bytes 4096 | tf_op jit(solution)/shard_map/all_to_all | solution.py:70
  20.5 88.7 %all-to-all-start = ((s32[1,8,4]{2,0,1:T(1,128)}), s32[1,8,4]{2,0,1:T(1,128)S(1)}, u32[]{:S(2)}, u32[]{:S(2)}) async-start(s32[1,8,4]{2,0,1:T(1,128)} %copy.53), calls=%async_computation | async-start | bytes 8192 | tf_op jit(solution)/shard_map/all_to_all | solution.py:67
  58.0 42.3 %copy-start.4 = (f32[16,128]{1,0:T(8,128)S(1)}, f32[16,128]{1,0:T(8,128)}, u32[]{:S(2)}) copy-start(f32[16,128]{1,0:T(8,128)} %param.20) | copy-start | bytes 24580
  58.0 42.3 %copy-start.8 = (f32[16]{0:T(128)S(1)}, f32[16]{0:T(128)}, u32[]{:S(2)}) copy-start(f32[16]{0:T(128)} %param.21) | copy-start | bytes 196
  100.3 13.6 %copy-start.5 = (s32[16,16]{1,0:T(8,128)S(1)}, s32[16,16]{1,0:T(8,128)}, u32[]{:S(2)}) copy-start(s32[16,16]{1,0:T(8,128)} %param.28) | copy-start | bytes 3076
  100.3 13.6 %copy-start.6 = (s32[16,16]{1,0:T(8,128)S(1)}, s32[16,16]{1,0:T(8,128)}, u32[]{:S(2)}) copy-start(s32[16,16]{1,0:T(8,128)} %param.29) | copy-start | bytes 3076
  109.2 19.5 %all-to-all-start.3 = ((bf16[4,4,128,128]{3,2,1,0:T(8,128)(2,1)}), bf16[4,4,128,128]{3,2,1,0:T(8,128)(2,1)S(1)}, u32[]{:S(2)}, u32[]{:S(2)}) async-start(bf16[4,4,128,128]{3,2,1,0:T(8,128)(2,1)} %bitcast.10), calls=%async_computation.3 | async-start | bytes 1048576 | tf_op jit(solution)/shard_map/all_to_all | solution.py:78
  128.7 33.1 %all-to-all-start.1 = ((bf16[8,4,128,128]{3,2,1,0:T(8,128)(2,1)}), bf16[8,4,128,128]{3,2,1,0:T(8,128)(2,1)S(1)}, u32[]{:S(2)}, u32[]{:S(2)}) async-start(bf16[8,4,128,128]{3,2,1,0:T(8,128)(2,1)} %bitcast.103), calls=%async_computation.1 | async-start | bytes 2097152 | tf_op jit(solution)/shard_map/all_to_all | solution.py:75
  132.7 8.6 %copy-start.9 = (f32[16,16]{1,0:T(8,128)S(1)}, f32[16,16]{1,0:T(8,128)}, u32[]{:S(2)}) copy-start(f32[16,16]{1,0:T(8,128)} %param.25) | copy-start | bytes 3076
  161.8 8.6 %copy-start.10 = (f32[16,16]{1,0:T(8,128)S(1)}, f32[16,16]{1,0:T(8,128)}, u32[]{:S(2)}) copy-start(f32[16,16]{1,0:T(8,128)} %param.24) | copy-start | bytes 3076
  170.5 32.2 %copy-start.2 = (f32[16,128,128]{2,1,0:T(8,128)S(1)}, f32[16,128,128]{2,1,0:T(8,128)}, u32[]{:S(2)}) copy-start(f32[16,128,128]{2,1,0:T(8,128)} %get-tuple-element.7) | copy-start | bytes 3145732
  170.5 40.2 %copy-start.7 = (s32[16,2]{0,1:T(2,128)S(1)}, s32[16,2]{0,1:T(2,128)}, u32[]{:S(2)}) copy-start(s32[16,2]{0,1:T(2,128)} %param.17) | copy-start | bytes 388
  207.2 18.8 %all-to-all-start.5 = ((bf16[4,4,128,128]{3,2,1,0:T(8,128)(2,1)}), bf16[4,4,128,128]{3,2,1,0:T(8,128)(2,1)S(1)}, u32[]{:S(2)}, u32[]{:S(2)}) async-start(bf16[4,4,128,128]{3,2,1,0:T(8,128)(2,1)} %bitcast.16), calls=%async_computation.5 | async-start | bytes 1048576 | tf_op jit(solution)/shard_map/all_to_all | solution.py:78
  226.0 33.0 %all-to-all-start.4 = ((bf16[8,4,128,128]{3,2,1,0:T(8,128)(2,1)}), bf16[8,4,128,128]{3,2,1,0:T(8,128)(2,1)S(1)}, u32[]{:S(2)}, u32[]{:S(2)}) async-start(bf16[8,4,128,128]{3,2,1,0:T(8,128)(2,1)} %bitcast.102), calls=%async_computation.4 | async-start | bytes 2097152 | tf_op jit(solution)/shard_map/all_to_all | solution.py:75
  229.9 203.4 %all-reduce.2.cloned.1.call-start = ((), (), s32[]{:S(2)}) async-start(), calls=%async_computation.8 | async-start | bytes 2097152 | tf_op jit(solution)/shard_map/psum | solution.py:119
  267.7 20.5 %copy-start.3 = (f32[16,128,128]{2,1,0:T(8,128)S(1)}, f32[16,128,128]{2,1,0:T(8,128)}, u32[]{:S(2)}) copy-start(f32[16,128,128]{2,1,0:T(8,128)} %get-tuple-element.7) | copy-start | bytes 3145732
  290.6 11.2 %copy-start.1 = (f32[16,128,128]{2,1,0:T(8,128)}, f32[16,128,128]{2,1,0:T(8,128)S(1)}, u32[]{:S(2)}) copy-start(f32[16,128,128]{2,1,0:T(8,128)S(1)} %divide_subtract_fusion) | copy-start | bytes 3145732
Sparse Core Ops, SparseCore 0:
  9.6 48.3 all-gather.2
  59.9 35.3 all-gather.4
  303.0 130.1 all-reduce.1
where the time goes:
time: 446 us; the launch traced here: 441 us
  waiting for transfers between devices  227 us (51%)
  matrix products  111 us (25%)
  local copies, waits for them, and re-layouts  55 us (12%)
  starting transfers between devices  26 us (6%)
  between operations  14.2 us (3%)
  other arithmetic  8.5 us (2%)
    psum x1, waiting for transfers between devices, body(): summed = lax.psum(partial_sum, ('ia', 'ja'))  130 us
    dot_general x4, matrix products, coupled(): jnp.einsum('pnac,pndc->pnad', left_side, margin_blocks, preferred_element...  93.8 us
    all_gather x1, waiting for transfers between devices, body(): row_slabs = lax.all_gather(slabs, 'ja', axis=0, tiled=True)  33.6 us
    all_gather x1, waiting for transfers between devices, body(): col_slabs = lax.all_gather(slabs, 'ia', axis=0, tiled=True)  32.9 us
    all_to_all x2, waiting for transfers between devices, body(): lax.all_to_all(sent[asked_cols], 'ja', split_axis=0, concat_axis=0, tiled...  25.9 us
    gather x2, local copies, waits for them, and re-layouts, body(): near_rows = table_rows[link_i]  17.3 us
    gather x2, local copies, waits for them, and re-layouts, body(): near_cols = table_cols[link_j]  17.3 us
  transfers between devices with their start and end apart: 9, of which 6 were waited for; matrix products, arithmetic and copies ran while one was open for 19% of the time, Pallas kernels for 0%

commit v1 on v0

--- a/solution.py
+++ b/solution.py
@@ -45,7 +45,12 @@
     col_peers = lax.axis_size("ja")
     row_slots = ask_i.shape[2]
     col_slots = ask_j.shape[2]
-    row_slabs = lax.all_gather(slabs, "ja", axis=0, tiled=True)
+    ring = [slabs]
+    for hop in range(3):
+        ring.append(lax.ppermute(ring[-1], "ja", [(dev, (dev + 1) % 4) for dev in range(4)]))
+    row_slabs = jnp.roll(
+        jnp.concatenate(ring[::-1], axis=0), (lax.axis_index("ja") + 1) * ring[0].shape[0], axis=0
+    )
     col_slabs = lax.all_gather(slabs, "ia", axis=0, tiled=True)
     rows_first = row_slabs.reshape(-1, BLK, aux_count)[
         pair_first[:, None] * block_count + dom_blocks

time: 446 us -> 408 us (0.915)
  waiting for transfers between devices: 227 us -> 187 us
    all_gather x1 -> x0, waiting for transfers between devices: 33.6 us -> none  [body(): row_slabs = lax.all_gather(slabs, 'ja', axis=0, tiled=True)]
    all_gather x1, waiting for transfers between devices: 32.9 us -> 0.01 us  [body(): col_slabs = lax.all_gather(slabs, 'ia', axis=0, tiled=True)]
    ppermute x0 -> x3, waiting for transfers between devices: none -> 27.6 us  [body(): lax.ppermute(ring[-1], 'ja', [(dev, (dev + 1) % 4) for dev in range(4)])]
    all_to_all x1, waiting for transfers between devices: 0.01 us -> 4.61 us  [body(): lax.all_to_all(ask_i, 'ia', split_axis=1, concat_axis=0, tiled=True)]
  transfers between devices with their start and end apart: 9 -> 11, of which waited for: 6 -> 7; matrix products, arithmetic and copies ran while one was open for 19% -> 18% of each run, Pallas kernels for 0% -> 0%
where the time goes in v1:
time: 408 us; the launch traced here: 402 us
  waiting for transfers between devices  187 us (46%)
  matrix products  111 us (27%)
  local copies, waits for them, and re-layouts  55.9 us (14%)
  starting transfers between devices  25.3 us (6%)
  between operations  14.5 us (4%)
  other arithmetic  8.5 us (2%)
    psum x1, waiting for transfers between devices, body(): summed = lax.psum(partial_sum, ('ia', 'ja'))  130 us
    dot_general x4, matrix products, coupled(): jnp.einsum('pnac,pndc->pnad', left_side, margin_blocks, preferred_element...  93.8 us
    ppermute x3, waiting for transfers between devices, body(): lax.ppermute(ring[-1], 'ja', [(dev, (dev + 1) % 4) for dev in range(4)])  27.6 us
    all_to_all x2, waiting for transfers between devices, body(): lax.all_to_all(sent[asked_cols], 'ja', split_axis=0, concat_axis=0, tiled...  23.7 us
    gather x2, local copies, waits for them, and re-layouts, body(): near_rows = table_rows[link_i]  17.3 us
    gather x2, local copies, waits for them, and re-layouts, body(): near_cols = table_cols[link_j]  17.3 us
  transfers between devices with their start and end apart: 11, of which 7 were waited for; matrix products, arithmetic and copies ran while one was open for 18% of the time, Pallas kernels for 0%

profile of v1, /device:TPU:0, one launch (start us, length us, event | category | flops | bytes accessed | tf_op | source)
XLA Modules:
  0.0 402.4 jit_solution(10152657278322399962)
XLA Ops:
  7.9 3.1 collective-permute-start
  11.0 3.9 all-to-all-start.2
  14.9 10.3 %collective-permute-done = bf16[1,512,512]{2,1,0:T(8,128)(2,1)S(1)} collective-permute-done((bf16[1,512,512]{2,1,0:T(8,128)(2,1)}, bf16[1,512,512]{2,1,0:T(8,128)(2,1)S(1)}, u32[]{:S(2)}, u32[]{:S(2)}) %collective-permute-start) | collective-permute-done | bytes 524320 | tf_op jit(solution)/shard_map/ppermute | solution.py:50
  28.3 11.8 %collective-permute-done.1 = bf16[1,512,512]{2,1,0:T(8,128)(2,1)S(1)} collective-permute-done((bf16[1,512,512]{2,1,0:T(8,128)(2,1)S(1)}, bf16[1,512,512]{2,1,0:T(8,128)(2,1)S(1)}, u32[]{:S(2)}, u32[]{:S(2)}) %collective-permute-start.1) | collective-permute-done | bytes 524320 | tf_op jit(solution)/shard_map/ppermute | solution.py:50
  40.1 3.5 all-to-all-start
  43.7 4.6 %all-to-all-done = s32[1,8,4]{2,0,1:T(1,128)S(1)} async-done(((s32[1,8,4]{2,0,1:T(1,128)}), s32[1,8,4]{2,0,1:T(1,128)S(1)}, u32[]{:S(2)}, u32[]{:S(2)}) %all-to-all-start) | async-done | bytes 160 | tf_op jit(solution)/shard_map/all_to_all | solution.py:72
  48.5 5.5 %collective-permute-done.2 = bf16[1,512,512]{2,1,0:T(8,128)(2,1)S(1)} collective-permute-done((bf16[1,512,512]{2,1,0:T(8,128)(2,1)S(1)}, bf16[1,512,512]{2,1,0:T(8,128)(2,1)S(1)}, u32[]{:S(2)}, u32[]{:S(2)}) %collective-permute-start.2) | collective-permute-done | bytes 524320 | tf_op jit(solution)/shard_map/ppermute | solution.py:50
  56.7 2.8 gather_fusion
  59.5 5.0 %gather_fusion.1 = bf16[32,128,512]{2,1,0:T(8,128)(2,1)} fusion(bf16[32,128,512]{2,1,0:T(8,128)(2,1)} %bitcast.98, s32[1024]{0:T(1024)S(1)} %pad_clamp_fusion.4), kind=kCustom, calls=%fused_computation.1 | custom fusion | bytes 8388736 | tf_op jit(solution)/shard_map/gather | solution.py:58
  64.5 7.5 %fusion.36 = (bf16[16,128,128]{2,1,0:T(8,128)(2,1)S(1)}, f32[16,128,128]{2,1,0:T(8,128)}) fusion(f32[16]{0:T(128)S(1)} %copy-done.8, f32[16,128]{1,0:T(8,128)S(1)} %copy-done.4, bf16[16,256,512]{2,1,0:T(8,128)(2,1)} %bitcast.100, bf16[16,256,128]{2,1,0:T(8,128)(2,1)S(1)} %copy-done, bf16[16,256,512]{2,1,0:T(8,128)(2,1)} %bitcast.99), kind=kOutput, calls=%fused_computation.44 | convolution fusion | flops 1345585152 | bytes 11018304 | tf_op jit(solution)/shard_map/paq,pbq->pab/dot_general | solution.py:67
  73.4 3.5 all-to-all-start.3
  77.1 1.7 gather_fusion.2
  78.8 10.5 %all-to-all-done.3 = bf16[4,4,128,128]{3,2,1,0:T(8,128)(2,1)S(1)} async-done(((bf16[4,4,128,128]{3,2,1,0:T(8,128)(2,1)}), bf16[4,4,128,128]{3,2,1,0:T(8,128)(2,1)S(1)}, u32[]{:S(2)}, u32[]{:S(2)}) %all-to-all-start.3) | async-done | bytes 524320 | tf_op jit(solution)/shard_map/all_to_all | solution.py:83
  89.3 3.9 all-to-all-start.1
  93.3 8.6 %gather_fusion.5 = bf16[256,128,128]{2,1,0:T(8,128)(2,1)} fusion(bf16[16,128,128]{2,1,0:T(8,128)(2,1)S(1)} %bitcast.88, s32[1024]{0:T(1024)S(1)} %pad_clamp_fusion), kind=kCustom, calls=%fused_computation.5 | custom fusion | bytes 16778240 | tf_op jit(solution)/shard_map/gather | solution.py:87
  101.9 20.5 %multiply_reduce_fusion.2 = f32[16,128,128]{2,1,0:T(8,128)} fusion(f32[16,16]{1,0:T(8,128)S(1)} %copy-done.9, bf16[16,16,128,128]{3,2,1,0:T(8,128)(2,1)} %param.23, bf16[16,16,128,128]{3,2,1,0:T(8,128)(2,1)} %bitcast.96), kind=kOutput, calls=%fused_computation.12 | convolution fusion | flops 2159804416 | bytes 17826816 | tf_op jit(solution)/shard_map/pnac,pndc->pnad/dot_general | solution.py:15
  122.4 8.6 %gather_fusion.3 = bf16[256,128,128]{2,1,0:T(8,128)(2,1)} fusion(bf16[32,128,128]{2,1,0:T(8,128)(2,1)S(1)} %bitcast.91, s32[1024]{0:T(1024)S(1)} %pad_clamp_fusion.2), kind=kCustom, calls=%fused_computation.3 | custom fusion | bytes 16778240 | tf_op jit(solution)/shard_map/gather | solution.py:86
  131.1 32.2 %multiply_reduce_fusion.3 = f32[16,128,128]{2,1,0:T(8,128)} fusion(f32[16,16]{1,0:T(8,128)S(1)} %copy-done.10, bf16[16,16,128,128]{3,2,1,0:T(8,128)(2,1)} %param.22, bf16[16,16,128,128]{3,2,1,0:T(8,128)(2,1)} %bitcast.97), kind=kOutput, calls=%fused_computation.13 | convolution fusion | flops 2159804416 | bytes 17826816 | tf_op jit(solution)/shard_map/pnac,pndc->pnad/dot_general | solution.py:15
  163.3 3.1 fusion.42
  167.9 3.5 all-to-all-start.5
  171.8 1.7 gather_fusion.6
  173.5 13.1 %all-to-all-done.5 = bf16[4,4,128,128]{3,2,1,0:T(8,128)(2,1)S(1)} async-done(((bf16[4,4,128,128]{3,2,1,0:T(8,128)(2,1)}), bf16[4,4,128,128]{3,2,1,0:T(8,128)(2,1)S(1)}, u32[]{:S(2)}, u32[]{:S(2)}) %all-to-all-start.5) | async-done | bytes 524320 | tf_op jit(solution)/shard_map/all_to_all | solution.py:83
  186.7 3.9 all-to-all-start.4
  190.6 8.6 %gather_fusion.9 = bf16[256,128,128]{2,1,0:T(8,128)(2,1)} fusion(bf16[16,128,128]{2,1,0:T(8,128)(2,1)S(1)} %bitcast.89, s32[1024]{0:T(1024)S(1)} %pad_clamp_fusion), kind=kCustom, calls=%fused_computation.9 | custom fusion | bytes 16778240 | tf_op jit(solution)/shard_map/gather | solution.py:87
  199.2 20.5 %multiply_reduce_fusion = f32[16,128,128]{2,1,0:T(8,128)} fusion(f32[16,16]{1,0:T(8,128)S(1)} %copy-done.9, bf16[16,16,128,128]{3,2,1,0:T(8,128)(2,1)} %param.23, bf16[16,16,128,128]{3,2,1,0:T(8,128)(2,1)} %bitcast.94), kind=kOutput, calls=%fused_computation.10 | convolution fusion | flops 2159804416 | bytes 17826816 | tf_op jit(solution)/shard_map/pnac,pndc->pnad/dot_general | solution.py:15
  219.7 8.6 %gather_fusion.7 = bf16[256,128,128]{2,1,0:T(8,128)(2,1)} fusion(bf16[32,128,128]{2,1,0:T(8,128)(2,1)S(1)} %bitcast.90, s32[1024]{0:T(1024)S(1)} %pad_clamp_fusion.2), kind=kCustom, calls=%fused_computation.7 | custom fusion | bytes 16778240 | tf_op jit(solution)/shard_map/gather | solution.py:86
  228.4 20.5 %multiply_reduce_fusion.1 = f32[16,128,128]{2,1,0:T(8,128)} fusion(f32[16,16]{1,0:T(8,128)S(1)} %copy-done.10, bf16[16,16,128,128]{3,2,1,0:T(8,128)(2,1)} %param.22, bf16[16,16,128,128]{3,2,1,0:T(8,128)(2,1)} %bitcast.95), kind=kOutput, calls=%fused_computation.11 | convolution fusion | flops 2159804416 | bytes 17826816 | tf_op jit(solution)/shard_map/pnac,pndc->pnad/dot_general | solution.py:15
  248.9 2.4 divide_subtract_fusion
  252.8 1.9 fusion.33
  256.0 1.9 fusion.43
  257.9 4.6 %fusion.16 = f32[4,4,128,128]{3,1,2,0:T(4,128)S(1)} fusion(f32[4,4,64,1]{1,2,3,0:T(8,128)S(1)} %bitcast.106, f32[8,8,128,128]{3,2,1,0:T(8,128)S(1)} %bitcast.93), kind=kOutput, calls=%fused_computation.28 | convolution fusion | flops 201326592 | bytes 5246976 | tf_op jit(solution)/shard_map/dot_general | solution.py:110
  263.6 130.3 %all-reduce.2.cloned.1.call-done = f32[512,512]{1,0:T(8,128)} async-done(((f32[512,512]{1,0:T(8,128)}), f32[512,512]{1,0:T(8,128)}) %all-reduce.2.cloned.1.call-update) | async-done | bytes 1048592 | tf_op jit(solution)/shard_map/psum | solution.py:124
  (73 shorter events, 15.5 us)
Async XLA Ops:
  7.2 57.3 %copy-start = (bf16[16,256,128]{2,1,0:T(8,128)(2,1)S(1)}, bf16[16,256,128]{2,1,0:T(8,128)(2,1)}, u32[]{:S(2)}) copy-start(bf16[16,256,128]{2,1,0:T(8,128)(2,1)} %param.16) | copy-start | bytes 3145732
  7.2 52.3 %all-gather.2.cloned.1.call-start = ((), (), s32[]{:S(2)}) async-start(), calls=%async_computation.6 | async-start | bytes 4718592 | tf_op jit(solution)/shard_map/all_gather | solution.py:54
  7.9 17.3 %collective-permute-start = (bf16[1,512,512]{2,1,0:T(8,128)(2,1)}, bf16[1,512,512]{2,1,0:T(8,128)(2,1)S(1)}, u32[]{:S(2)}, u32[]{:S(2)}) collective-permute-start(bf16[1,512,512]{2,1,0:T(8,128)(2,1)} %param.15), channel_id=1, source_target_pairs={{0,1},{1,2},{2,3},{3,0},{4,5},{5,6},{6,7},{7,4},{8,9},{9,10},{10,1... | collective-permute-start | bytes 1572872 | tf_op jit(solution)/shard_map/ppermute | solution.py:50
  11.0 29.1 %all-to-all-start.2 = ((s32[1,4,4]{2,0,1:T(1,128)}), s32[1,4,4]{2,0,1:T(1,128)S(1)}, u32[]{:S(2)}, u32[]{:S(2)}) async-start(s32[1,4,4]{2,0,1:T(1,128)} %bitcast.108), calls=%async_computation.2 | async-start | bytes 4096 | tf_op jit(solution)/shard_map/all_to_all | solution.py:75
  25.2 14.9 %collective-permute-start.1 = (bf16[1,512,512]{2,1,0:T(8,128)(2,1)S(1)}, bf16[1,512,512]{2,1,0:T(8,128)(2,1)S(1)}, u32[]{:S(2)}, u32[]{:S(2)}) collective-permute-start(bf16[1,512,512]{2,1,0:T(8,128)(2,1)S(1)} %collective-permute-done), channel_id=1, source_target_pairs={{0,1},{1,2},{2,3},{3,0},{4,5},{5,6},{6,7},{7,4},{8,9},{9,10},{10,1... | collective-permute-start | bytes 1572872 | tf_op jit(solution)/shard_map/ppermute | solution.py:50
  40.1 14.0 %collective-permute-start.2 = (bf16[1,512,512]{2,1,0:T(8,128)(2,1)S(1)}, bf16[1,512,512]{2,1,0:T(8,128)(2,1)S(1)}, u32[]{:S(2)}, u32[]{:S(2)}) collective-permute-start(bf16[1,512,512]{2,1,0:T(8,128)(2,1)S(1)} %collective-permute-done.1), channel_id=1, source_target_pairs={{0,1},{1,2},{2,3},{3,0},{4,5},{5,6},{6,7},{7,4},{8,9},{9,10},{10,1... | collective-permute-start | bytes 1572872 | tf_op jit(solution)/shard_map/ppermute | solution.py:50
  40.1 8.2 %all-to-all-start = ((s32[1,8,4]{2,0,1:T(1,128)}), s32[1,8,4]{2,0,1:T(1,128)S(1)}, u32[]{:S(2)}, u32[]{:S(2)}) async-start(s32[1,8,4]{2,0,1:T(1,128)} %copy.53), calls=%async_computation | async-start | bytes 8192 | tf_op jit(solution)/shard_map/all_to_all | solution.py:72
  56.6 7.8 %copy-start.4 = (f32[16,128]{1,0:T(8,128)S(1)}, f32[16,128]{1,0:T(8,128)}, u32[]{:S(2)}) copy-start(f32[16,128]{1,0:T(8,128)} %param.20) | copy-start | bytes 24580
  56.7 7.8 %copy-start.8 = (f32[16]{0:T(128)S(1)}, f32[16]{0:T(128)}, u32[]{:S(2)}) copy-start(f32[16]{0:T(128)} %param.21) | copy-start | bytes 196
  64.5 12.4 %copy-start.5 = (s32[16,16]{1,0:T(8,128)S(1)}, s32[16,16]{1,0:T(8,128)}, u32[]{:S(2)}) copy-start(s32[16,16]{1,0:T(8,128)} %param.28) | copy-start | bytes 3076
  64.5 12.5 %copy-start.6 = (s32[16,16]{1,0:T(8,128)S(1)}, s32[16,16]{1,0:T(8,128)}, u32[]{:S(2)}) copy-start(s32[16,16]{1,0:T(8,128)} %param.29) | copy-start | bytes 3076
  73.4 15.9 %all-to-all-start.3 = ((bf16[4,4,128,128]{3,2,1,0:T(8,128)(2,1)}), bf16[4,4,128,128]{3,2,1,0:T(8,128)(2,1)S(1)}, u32[]{:S(2)}, u32[]{:S(2)}) async-start(bf16[4,4,128,128]{3,2,1,0:T(8,128)(2,1)} %bitcast.10), calls=%async_computation.3 | async-start | bytes 1048576 | tf_op jit(solution)/shard_map/all_to_all | solution.py:83
  89.3 33.1 %all-to-all-start.1 = ((bf16[8,4,128,128]{3,2,1,0:T(8,128)(2,1)}), bf16[8,4,128,128]{3,2,1,0:T(8,128)(2,1)S(1)}, u32[]{:S(2)}, u32[]{:S(2)}) async-start(bf16[8,4,128,128]{3,2,1,0:T(8,128)(2,1)} %bitcast.103), calls=%async_computation.1 | async-start | bytes 2097152 | tf_op jit(solution)/shard_map/all_to_all | solution.py:80
  93.3 8.7 %copy-start.9 = (f32[16,16]{1,0:T(8,128)S(1)}, f32[16,16]{1,0:T(8,128)}, u32[]{:S(2)}) copy-start(f32[16,16]{1,0:T(8,128)} %param.25) | copy-start | bytes 3076
  122.4 8.6 %copy-start.10 = (f32[16,16]{1,0:T(8,128)S(1)}, f32[16,16]{1,0:T(8,128)}, u32[]{:S(2)}) copy-start(f32[16,16]{1,0:T(8,128)} %param.24) | copy-start | bytes 3076
  131.1 32.2 %copy-start.2 = (f32[16,128,128]{2,1,0:T(8,128)S(1)}, f32[16,128,128]{2,1,0:T(8,128)}, u32[]{:S(2)}) copy-start(f32[16,128,128]{2,1,0:T(8,128)} %get-tuple-element.7) | copy-start | bytes 3145732
  131.1 40.3 %copy-start.7 = (s32[16,2]{0,1:T(2,128)S(1)}, s32[16,2]{0,1:T(2,128)}, u32[]{:S(2)}) copy-start(s32[16,2]{0,1:T(2,128)} %param.17) | copy-start | bytes 388
  167.9 18.8 %all-to-all-start.5 = ((bf16[4,4,128,128]{3,2,1,0:T(8,128)(2,1)}), bf16[4,4,128,128]{3,2,1,0:T(8,128)(2,1)S(1)}, u32[]{:S(2)}, u32[]{:S(2)}) async-start(bf16[4,4,128,128]{3,2,1,0:T(8,128)(2,1)} %bitcast.16), calls=%async_computation.5 | async-start | bytes 1048576 | tf_op jit(solution)/shard_map/all_to_all | solution.py:83
  186.7 33.1 %all-to-all-start.4 = ((bf16[8,4,128,128]{3,2,1,0:T(8,128)(2,1)}), bf16[8,4,128,128]{3,2,1,0:T(8,128)(2,1)S(1)}, u32[]{:S(2)}, u32[]{:S(2)}) async-start(bf16[8,4,128,128]{3,2,1,0:T(8,128)(2,1)} %bitcast.102), calls=%async_computation.4 | async-start | bytes 2097152 | tf_op jit(solution)/shard_map/all_to_all | solution.py:80
  190.5 203.4 %all-reduce.2.cloned.1.call-start = ((), (), s32[]{:S(2)}) async-start(), calls=%async_computation.7 | async-start | bytes 2097152 | tf_op jit(solution)/shard_map/psum | solution.py:124
  228.4 20.5 %copy-start.3 = (f32[16,128,128]{2,1,0:T(8,128)S(1)}, f32[16,128,128]{2,1,0:T(8,128)}, u32[]{:S(2)}) copy-start(f32[16,128,128]{2,1,0:T(8,128)} %get-tuple-element.7) | copy-start | bytes 3145732
  251.3 11.2 %copy-start.1 = (f32[16,128,128]{2,1,0:T(8,128)}, f32[16,128,128]{2,1,0:T(8,128)S(1)}, u32[]{:S(2)}) copy-start(f32[16,128,128]{2,1,0:T(8,128)S(1)} %divide_subtract_fusion) | copy-start | bytes 3145732
Sparse Core Ops, SparseCore 0:
  9.9 39.3 all-gather.1
  263.7 130.1 all-reduce.1
